TPU v7x, 32 devices: a whole 2x2x4 slice. The times are simulated.
32 devices in a mesh: row: 8 (over y, x, core), col: 4 (over z).
Axes of the slice: x: 2, y: 2, z: 4, core: 2. Of those that a mesh axis runs over, the one named last changes fastest.
Arguments:
- source_features: bfloat16 [4, 2048, 256], P('col', 'row'), may hold values from -500 to 500
- target_features: bfloat16 [8192, 256], P(('row', 'col')), may hold values from -6 to 6
- weight: bfloat16 [256, 256], replicated, may hold values from -0.375 to 0.375
- score_source: float32 [4, 64], replicated, may hold values from -0.75 to 0.75
- score_target: float32 [4, 64], replicated, may hold values from -0.75 to 0.75
- out_bias: float32 [256], replicated, may hold values from -3 to 3
- block_list: int32 [8, 4, 48], P('row', 'col'), may hold values from 0 to 127, as said below
- block_count: int32 [8, 4], P('row', 'col'), may hold values from 8 to 48, as said below
- edge_bits: int32 [8, 4, 48, 16, 128], P('row', 'col'), may hold values from 0 to 255, as said below
Outputs:
- updated: bfloat16 [8192, 256], P(('row', 'col'))
Inputs may be any that keep to these rules, and one draw needn't show every extreme that they name: `block_list`: slot s of tile (r, c) names target block p // 16 and source block p % 16 of the tile; the first block_count[r, c] slots of a tile name distinct blocks and later slots are unused. `block_count`: some tile holds 48 blocks. `edge_bits`: bit b of entry [r, c, s, w, i] marks the edge from source 8 w + b to target i of the block in slot s. Some targets have no edge.
All inputs are finite; a program needn't handle non-finite values.
Results may differ from a plain program's by a relative error of at most 0.007.
The roundings to bfloat16 on the way count: a program that leaves them out, or rounds other values in their place, can miss the bound.
Values may be sent and summed in bfloat16 or wider, within the bound.
No kernel may reach another device: no remote copies, remote signals or barrier semaphores. Data moves between devices by JAX's collectives and lax.ppermute only.
A program may use at most 64 MiB of HBM per device.

v0:
```python
import jax
import jax.numpy as jnp
from jax import lax
from jax.sharding import PartitionSpec as P

BLK = 128
SB = 16


very_low = -1e30
slope = 0.2


def unpack_all(packed):
    shifts = jnp.arange(8, dtype=jnp.int32)
    spread = jnp.right_shift(packed[:, :, None, :], shifts[None, None, :, None]) & 1
    return spread.reshape(packed.shape[0], packed.shape[1] * 8, packed.shape[2]) > 0


def all_scores(src_pick, dst_pick):
    raw = src_pick[:, :, :, None] + dst_pick[:, :, None, :]
    return jnp.where(raw > 0, raw, slope * raw)


def body(
    source_features,
    target_features,
    weight,
    score_source,
    score_target,
    out_bias,
    block_list,
    block_count,
    edge_bits,
):
    head_count = score_source.shape[0]
    head_size = score_source.shape[1]
    out_width = weight.shape[1]
    own_proj = jnp.dot(source_features[0], weight, preferred_element_type=jnp.float32).astype(
        jnp.bfloat16
    )
    projected = lax.all_gather(own_proj, "row", axis=0, tiled=True)
    src_logits = jnp.einsum(
        "nhk,hk->hn",
        projected.reshape(-1, head_count, head_size).astype(jnp.float32),
        score_source,
        precision=lax.Precision.HIGHEST,
    )
    dst_proj = jnp.dot(target_features, weight, preferred_element_type=jnp.float32)
    dst_local = jnp.einsum(
        "nhk,hk->hn",
        dst_proj.reshape(-1, head_count, head_size),
        score_target,
        precision=lax.Precision.HIGHEST,
    )
    dst_logits = lax.all_gather(dst_local, "col", axis=1, tiled=True)
    dst_rows = dst_logits.shape[1]
    dst_blocks_all = dst_rows // BLK
    src_blocks_all = src_logits.shape[1] // BLK
    slots = block_list[0, 0]
    live = block_count[0, 0]
    packed = edge_bits[0, 0]
    slot_count = slots.shape[0]
    dst_block = slots // SB
    src_block = slots % SB
    in_use = jnp.arange(slot_count, dtype=jnp.int32) < live
    edge_mask = unpack_all(packed) & in_use[:, None, None]
    src_pick = jnp.take(src_logits.reshape(head_count, src_blocks_all, BLK), src_block, axis=1)
    dst_pick = jnp.take(dst_logits.reshape(head_count, dst_blocks_all, BLK), dst_block, axis=1)
    owner = dst_block[:, None] == jnp.arange(dst_blocks_all, dtype=jnp.int32)[None, :]
    owner_float = owner.astype(jnp.float32)
    scores = all_scores(src_pick, dst_pick)
    block_max = jnp.max(jnp.where(edge_mask[None], scores, very_low), axis=2)
    spread_max = jnp.where(owner[None, :, :, None], block_max[:, :, None, :], very_low)
    row_max = jnp.max(spread_max, axis=1).reshape(head_count, dst_rows)
    row_max = lax.pmax(row_max, "col")
    prior_max = jnp.take(row_max.reshape(head_count, dst_blocks_all, BLK), dst_block, axis=1)
    scores = all_scores(src_pick, dst_pick)
    numer = jnp.exp(jnp.where(edge_mask[None], scores - prior_max[:, :, None, :], very_low))
    slot_denoms = jnp.sum(numer, axis=2)
    denoms = jnp.einsum(
        "sd,hsi->dih", owner_float, slot_denoms, precision=lax.Precision.HIGHEST
    ).reshape(dst_rows, head_count)
    weights = numer.astype(jnp.bfloat16)
    src_feats = jnp.take(
        projected.reshape(src_blocks_all, BLK, head_count, head_size), src_block, axis=0
    )
    product = jnp.einsum("hsji,sjhk->sihk", weights, src_feats, preferred_element_type=jnp.float32)
    accum = jnp.einsum(
        "sd,sihk->dihk", owner_float, product, precision=lax.Precision.HIGHEST
    ).reshape(dst_rows, out_width)
    accum, denoms = (
        lax.psum(accum.astype(jnp.bfloat16), "col").astype(jnp.float32),
        lax.psum(denoms.astype(jnp.bfloat16), "col").astype(jnp.float32),
    )
    own_count = dst_rows // lax.axis_size("col")
    first_row = lax.axis_index("col") * own_count
    accum = lax.dynamic_slice_in_dim(accum, first_row, own_count, 0)
    denoms = lax.dynamic_slice_in_dim(denoms, first_row, own_count, 0)
    own_count = accum.shape[0]
    blended = accum.reshape(own_count, head_count, head_size) / jnp.maximum(denoms, 1.0)[:, :, None]
    return jax.nn.elu(blended.reshape(own_count, out_width) + out_bias).astype(jnp.bfloat16)


def solution(mesh):
    placed = (
        P("col", "row", None),
        P(("row", "col"), None),
        P(),
        P(),
        P(),
        P(),
        P("row", "col", None),
        P("row", "col"),
        P("row", "col", None, None, None),
    )
    return jax.shard_map(
        body, mesh=mesh, in_specs=placed, out_specs=P(("row", "col"), None), check_vma=False
    )
```

profile of v0, /device:TPU:0, one launch (start us, length us, event | category | flops | bytes accessed | tf_op | source)
XLA Modules:
  0.0 129.9 jit_solution(5069399129637449960)
XLA Ops:
  6.5 0.0 copy-start
  6.5 0.0 all-gather.2.cloned.1.call-start
  6.5 0.9 copy-done
  7.4 1.7 %convolution_convert_fusion = bf16[256,256]{1,0:T(8,128)(2,1)} fusion(bf16[256,256]{1,0:T(8,128)(2,1)S(1)} %copy-done, bf16[1,256,256]{2,1,0:T(8,128)(2,1)} %param.11), kind=kOutput, calls=%fused_computation.28 | convolution fusion | flops 33619968 | bytes 393216 | tf_op jit(solution)/shard_map/dot_general | solution.py:39
  9.2 0.0 all-gather.2.cloned.1.call-update
  9.2 0.0 all-reduce.2.cloned.1.call-start
  9.3 1.1 fusion.44
  10.4 0.9 fusion.45
  11.4 0.1 shift_right_arithmetic.30
  12.1 0.7 compare_and_fusion
  12.8 0.1 copy.37
  12.9 14.9 %all_gather.7 = f32[4,1024]{1,0:T(4,128)S(1)} all-gather(f32[4,256]{1,0:T(4,128)S(1)} %bitcast.103), channel_id=1, replica_groups=mesh['row'=8,'col'=4] {'col'}, dimensions={1}, use_global_device_ids=true | all-gather | bytes 20480 | tf_op jit(solution)/shard_map/all_gather | solution.py:56
  27.8 0.6 gather_fusion.2
  28.5 0.7 fusion.38
  29.2 1.9 %fusion.17 = pred[48,128,128]{2,1,0:T(8,128)(4,1)S(1)} fusion(s32[128]{0:T(128)S(1)} %shift_right_arithmetic.30, s32[48,16,128]{2,1,0:T(8,128)} %bitcast.101, pred[48]{0:T(512)(128)(4,1)S(1)} %iota_compare_fusion.3), kind=kLoop, calls=%fused_computation.24 | loop fusion | flops 3145728 | bytes 1180208 | tf_op jit(solution)/shard_map/and | solution.py:67
  31.1 0.0 copy-start.2
  31.1 4.4 %all-gather.2.cloned.1.call-done = bf16[2048,256]{1,0:T(8,128)(2,1)} async-done(((bf16[256,256]{1,0:T(8,128)(2,1)}), bf16[2048,256]{1,0:T(8,128)(2,1)}) %all-gather.2.cloned.1.call-update) | async-done | bytes 1048592 | tf_op jit(solution)/shard_map/all_gather | solution.py:42
  35.5 0.0 copy-start.1
  35.5 1.6 %copy.36 = bf16[2048,256]{0,1:T(8,128)(2,1)S(1)} copy(bf16[2048,256]{1,0:T(8,128)(2,1)} %all-gather.2.cloned.1.call-done) | data formatting | bytes 2097152 | tf_op jit(solution)/shard_map/all_gather | solution.py:42
  37.0 1.2 fusion.43
  38.3 0.6 gather_fusion.1
  38.9 0.2 select_bitcast_fusion.1
  39.1 4.4 %select_reduce_fusion = f32[4,48,128]{2,0,1:T(4,128)S(1)} fusion(f32[4,48,128]{2,0,1:T(4,128)S(1)} %get-tuple-element.9, f32[4,48,128]{2,0,1:T(4,128)S(1)} %get-tuple-element.10, pred[48,128,128]{2,1,0:T(8,128)(4,1)S(1)} %fusion.17), kind=kLoop, calls=%fused_computation.6 | loop fusion | flops 18849792 | bytes 1081344 | tf_op jit(solution)/shard_map/reduce_max | solution.py:73
  43.5 0.1 select_reduce_fusion.1
  43.6 18.7 %pmax.7 = f32[4,8,128]{2,0,1:T(4,128)S(1)} all-reduce(f32[4,8,128]{2,0,1:T(4,128)S(1)} %copy.39), channel_id=1, replica_groups=mesh['row'=8,'col'=4] {'col'}, use_global_device_ids=true, to_apply=%region_2.4 | all-reduce | flops 4096 | bytes 32768 | tf_op jit(solution)/shard_map/pmax | solution.py:76
  62.4 0.6 gather_fusion.3
  63.0 0.0 copy-done.2
  63.0 0.8 select_bitcast_fusion
  63.8 0.0 copy-done.1
  63.8 0.8 reshape.226
  64.6 1.1 copy.35
  65.7 0.0 copy-start.3
  65.7 0.0 copy-start.4
  65.7 2.7 %gather_fusion = bf16[48,128,4,64]{1,3,2,0:T(8,128)(2,1)} fusion(bf16[16,128,4,64]{1,3,2,0:T(8,128)(2,1)S(1)} %copy.35, s32[1024]{0:T(1024)S(1)} %pad_clamp_fusion.1), kind=kCustom, calls=%fused_computation.2 | custom fusion | bytes 6291648 | tf_op jit(solution)/shard_map/jit(_take)/gather | solution.py:85
  68.4 0.0 copy-done.3
  68.4 0.0 copy-done.4
  68.4 9.9 %fusion.18 = f32[48,128,4,64]{1,3,2,0:T(8,128)S(1)} fusion(f32[4,48,128]{2,0,1:T(4,128)S(1)} %copy-done.4, f32[4,48,128]{2,0,1:T(4,128)S(1)} %get-tuple-element.9, f32[4,48,128]{2,0,1:T(4,128)S(1)} %get-tuple-element.10, pred[48,128,128]{2,1,0:T(8,128)(4,1)S(1)} %copy-done.3, bf16[48,128,4,64]{1,3,2,0:T(8,128)(2,1)} %gather_fusion, ...), kind=kOutput, calls=%fused_computation.25 | convolution fusion | flops 426246144 | bytes 10518576 | tf_op jit(solution)/shard_map/hsji,sjhk->sihk/dot_general | solution.py:88
  78.3 0.0 copy-start.5
  78.4 5.7 %fusion.24 = bf16[8,128,4,64]{1,0,3,2:T(8,128)(2,1)S(1)} fusion(f32[48,128,4,64]{1,3,2,0:T(8,128)S(1)} %fusion.18, s32[48]{0:T(128)S(1)} %get-tuple-element.7), kind=kOutput, calls=%fused_computation.27 | convolution fusion | flops 151257472 | bytes 6815936 | tf_op jit(solution)/shard_map/sd,sihk->dihk/dot_general | solution.py:89
  84.0 0.9 copy.62
  84.9 0.0 all-reduce.2.cloned.1.call-update
  85.0 5.5 %fusion = f32[4,48,128]{2,0,1:T(4,128)S(1)} fusion(f32[4,48,128]{2,0,1:T(4,128)S(1)} %copy-done.4, f32[4,48,128]{2,0,1:T(4,128)S(1)} %get-tuple-element.9, f32[4,48,128]{2,0,1:T(4,128)S(1)} %get-tuple-element.10, pred[48,128,128]{2,1,0:T(8,128)(4,1)S(1)} %copy-done.3), kind=kLoop, calls=%fused_computation.7 | loop fusion | flops 21995520 | bytes 1179648 | tf_op jit(solution)/shard_map/reduce_sum | solution.py:80
  90.5 0.2 fusion.27
  90.6 8.8 %psum.15 = bf16[1024,4]{0,1:T(4,128)(2,1)S(1)} all-reduce(bf16[1024,4]{0,1:T(4,128)(2,1)S(1)} %bitcast.102), channel_id=1, replica_groups=mesh['row'=8,'col'=4] {'col'}, use_global_device_ids=true, to_apply=%region_5.7 | all-reduce | flops 4096 | bytes 16384 | tf_op jit(solution)/shard_map/psum | solution.py:94
  99.5 21.7 %all-reduce.2.cloned.1.call-done = bf16[1024,256]{0,1:T(8,128)(2,1)} async-done(((bf16[1024,256]{0,1:T(8,128)(2,1)}), bf16[1024,256]{0,1:T(8,128)(2,1)}) %all-reduce.2.cloned.1.call-update) | async-done | bytes 524304 | tf_op jit(solution)/shard_map/psum | solution.py:93
  121.2 0.0 copy-done.5
  121.2 1.1 fusion.29
  122.3 0.8 copy.42
  (12 shorter events, 0.1 us)
Async XLA Ops:
  6.5 0.9 copy-start
  6.5 28.9 %all-gather.2.cloned.1.call-start = ((), (), s32[]{:S(2)}) async-start(), calls=%async_computation | async-start | bytes 1179648 | tf_op jit(solution)/shard_map/all_gather | solution.py:42
  9.2 112.0 %all-reduce.2.cloned.1.call-start = ((), (), s32[]{:S(2)}) async-start(), calls=%async_computation.1 | async-start | bytes 1048576 | tf_op jit(solution)/shard_map/psum | solution.py:93
  31.1 31.9 %copy-start.2 = (pred[48,128,128]{2,1,0:T(8,128)(4,1)}, pred[48,128,128]{2,1,0:T(8,128)(4,1)S(1)}, u32[]{:S(2)}) copy-start(pred[48,128,128]{2,1,0:T(8,128)(4,1)S(1)} %fusion.17) | copy-start | bytes 2359300
  35.5 28.3 %copy-start.1 = (bf16[2048,256]{1,0:T(8,128)(2,1)S(1)}, bf16[2048,256]{1,0:T(8,128)(2,1)}, u32[]{:S(2)}) copy-start(bf16[2048,256]{1,0:T(8,128)(2,1)} %all-gather.2.cloned.1.call-done) | copy-start | bytes 3145732
  65.7 2.7 %copy-start.3 = (pred[48,128,128]{2,1,0:T(8,128)(4,1)S(1)}, pred[48,128,128]{2,1,0:T(8,128)(4,1)}, u32[]{:S(2)}) copy-start(pred[48,128,128]{2,1,0:T(8,128)(4,1)} %copy-done.2) | copy-start | bytes 2359300
  65.7 2.7 %copy-start.4 = (f32[4,48,128]{2,0,1:T(4,128)S(1)}, f32[4,48,128]{2,0,1:T(4,128)}, u32[]{:S(2)}) copy-start(f32[4,48,128]{2,0,1:T(4,128)} %select_bitcast_fusion) | copy-start | bytes 294916
  78.3 42.8 %copy-start.5 = (f32[256]{0:T(256)S(1)}, f32[256]{0:T(256)}, u32[]{:S(2)}) copy-start(f32[256]{0:T(256)} %param.16) | copy-start | bytes 3076
Sparse Core Ops, SparseCore 0:
  9.3 26.0 all-gather.1
  85.1 36.0 all-reduce.1
where the time goes:
time: 130 us
  blocking collectives  42.5 us (33%)
  waiting for transfers between devices  26.1 us (20%)
  matrix products  20.7 us (16%)
  other arithmetic  15.3 us (12%)
  between operations  14.3 us (11%)
  local copies, waits for them, and re-layouts  10.9 us (8%)
    psum x1, waiting for transfers between devices, body(): lax.psum(accum.astype(jnp.bfloat16), 'col').astype(jnp.float32)  21.7 us
    pmax x1, blocking collectives, body(): row_max = lax.pmax(row_max, 'col')  18.7 us
    all_gather x1, blocking collectives, body(): dst_logits = lax.all_gather(dst_local, 'col', axis=1, tiled=True)  14.9 us
    dot_general x1, matrix products, body(): jnp.einsum('hsji,sjhk->sihk', weights, src_feats, preferred_element_type=...  9.89 us
    psum x1, blocking collectives, body(): lax.psum(denoms.astype(jnp.bfloat16), 'col').astype(jnp.float32)  8.82 us
    dot_general x1, matrix products, body(): jnp.einsum('sd,sihk->dihk', owner_float, product, precision=lax.Precision...  5.67 us
    reduce_sum x1, other arithmetic, body(): slot_denoms = jnp.sum(numer, axis=2)  5.5 us
    reduce_max x1, other arithmetic, body(): block_max = jnp.max(jnp.where(edge_mask[None], scores, very_low), axis=2)  4.36 us
  transfers between devices with their start and end apart: 2, of which 2 were waited for; matrix products, arithmetic and copies ran while one was open for 9% of the time, Pallas kernels for 0%

commit v1 on v0

v1 whole, which is shorter than its diff:
```python
import functools

import jax
import jax.numpy as jnp
from jax import lax
from jax.experimental import pallas as pl
from jax.experimental.pallas import tpu as pltpu
from jax.sharding import PartitionSpec as P

BLK = 128
GROUP = 4
very_low = -1e30
slope = 0.2
log2e = 1.4426950408889634
f32 = jnp.float32
bf16 = jnp.bfloat16
NT = (((1,), (1,)), ((), ()))


def leaky(z):
    return jnp.maximum(z, slope * z)


def block_rows(scores, width):
    heads, size = scores.shape
    tiled = jnp.concatenate([scores] * heads, axis=1)
    row = lax.broadcasted_iota(jnp.int32, tiled.shape, 0)
    column = lax.broadcasted_iota(jnp.int32, tiled.shape, 1)
    return jnp.where(column // size == row, tiled, 0.0)


def thirds(value):
    high = value.astype(bf16)
    rest = value - high.astype(f32)
    middle = rest.astype(bf16)
    low = (rest - middle.astype(f32)).astype(bf16)
    return high, middle, low


def target_kernel(x_ref, w_ref, score_ref, out_ref):
    rows = block_rows(score_ref[...], w_ref.shape[1])
    product = jnp.dot(x_ref[...], w_ref[...], preferred_element_type=f32)
    logits = lax.dot_general(
        rows, product, NT, precision=lax.Precision.HIGHEST, preferred_element_type=f32
    )
    out_ref[...] = logits * log2e


def tile_kernel(cfg, *refs):
    heads, size, src_blocks, dst_blocks, n_src, n_dst, row_axis, col_axis, split = cfg
    refs = list(refs)
    slots_ref, count_ref, bits_ref, w_ref, score_ref = refs[:5]
    x_refs = refs[5 : 5 + n_src]
    d_refs = refs[5 + n_src : 5 + n_src + n_dst]
    n_out = n_dst if split else 1
    out_refs = refs[5 + n_src + n_dst : 5 + n_src + n_dst + n_out]
    feats, spread, logit, top, total, accum = refs[5 + n_src + n_dst + n_out :]
    width = w_ref.shape[1]

    turned = w_ref[...].astype(f32).T.astype(bf16)
    parts = thirds(block_rows(score_ref[...], width))
    rows = jnp.concatenate([part.astype(f32) for part in parts], axis=0).astype(bf16)
    for k in range(n_src):
        x = x_refs[k][...]
        x = x.reshape(x.shape[-2], x.shape[-1])
        blocks = x.shape[0] // BLK
        first = (lax.axis_index(row_axis) ^ k) * blocks if n_src > 1 else 0
        projected = jnp.dot(x, w_ref[...], preferred_element_type=f32).astype(bf16)
        three = lax.dot_general(projected, rows, NT, preferred_element_type=f32)
        source = three[:, :heads] + three[:, heads : 2 * heads] + three[:, 2 * heads : 3 * heads]
        source = source * log2e
        across = lax.dot_general(turned, x, NT, preferred_element_type=f32).astype(bf16)
        for b in range(blocks):
            feats[first + b] = across[:, b * BLK : (b + 1) * BLK]
            for h in range(heads):
                column = source[b * BLK : (b + 1) * BLK, h : h + 1]
                spread[(first + b) * heads + h] = jnp.broadcast_to(column, (BLK, BLK))
    for k in range(n_dst):
        d = d_refs[k][...]
        blocks = d.shape[1] // BLK
        first = (lax.axis_index(col_axis) ^ k) * blocks if n_dst > 1 else 0
        for b in range(blocks):
            logit[first + b] = d[:, b * BLK : (b + 1) * BLK]
    top[...] = jnp.full(top.shape, very_low, f32)
    total[...] = jnp.zeros(total.shape, f32)
    accum[...] = jnp.zeros(accum.shape, f32)

    live = count_ref[0, 0]
    groups = (live + GROUP - 1) // GROUP
    bit = jnp.left_shift(1, lax.broadcasted_iota(jnp.int32, (1, 8, BLK), 1))

    def place(slot):
        p = slots_ref[0, 0, slot]
        return p // src_blocks, p % src_blocks

    def edges(slot):
        packed = jnp.where(slot < live, bits_ref[0, 0, slot], 0)
        return (packed[:, None, :] & bit) != 0

    def largest(group, carry):
        found = []
        for member in range(GROUP):
            slot = group * GROUP + member
            dst, src = place(slot)
            mask = edges(slot)
            for h in range(heads):
                s = spread[src * heads + h].reshape(BLK // 8, 8, BLK)
                found.append((dst, h, jnp.max(jnp.where(mask, s, very_low), axis=0)))
        for dst, h, value in found:
            top[dst * heads + h] = jnp.maximum(top[dst * heads + h], value)
        return carry

    lax.fori_loop(0, groups, largest, 0)

    for b in range(dst_blocks):
        best = [jnp.max(top[b * heads + h], axis=0, keepdims=True) for h in range(heads)]
        z = jnp.concatenate(best, axis=0) + logit[b]
        top[b * heads, :heads] = leaky(z)

    def gather(group, carry):
        sums = []
        for member in range(GROUP):
            slot = group * GROUP + member
            dst, src = place(slot)
            mask = edges(slot)
            feat = feats[src]
            products = []
            for h in range(heads):
                s = spread[src * heads + h].reshape(BLK // 8, 8, BLK)
                d = logit[dst, h : h + 1].reshape(1, 1, BLK)
                m = top[dst * heads, h : h + 1].reshape(1, 1, BLK)
                e = jnp.exp2(jnp.where(mask, leaky(s + d) - m, very_low))
                sums.append((dst, h, jnp.sum(e, axis=0)))
                weights = e.reshape(BLK, BLK).astype(bf16)
                products.append(
                    jnp.dot(
                        feat[h * size : (h + 1) * size],
                        weights,
                        preferred_element_type=f32,
                    )
                )
            sums.append((dst, -1, products))
        for dst, h, value in sums:
            if h >= 0:
                total[dst * heads + h] = total[dst * heads + h] + value
            else:
                for g in range(heads):
                    part = pl.ds(g * size, size)
                    accum[dst, part] = accum[dst, part] + value[g]
        return carry

    lax.fori_loop(0, groups, gather, 0)

    def write(out_ref, lanes, b):
        out_ref[:width, lanes] = accum[b].astype(bf16)
        m = top[b * heads, :heads]
        denom = [jnp.sum(total[b * heads + h], axis=0, keepdims=True) for h in range(heads)]
        stats = [part.astype(f32) for part in thirds(m)] + denom
        out_ref[width:, lanes] = jnp.concatenate(stats, axis=0).astype(bf16)

    if split:
        blocks = dst_blocks // n_dst
        for k in range(n_dst):
            first = (lax.axis_index(col_axis) ^ k) * blocks
            for b in range(blocks):
                write(out_refs[k], pl.ds(b * BLK, BLK), first + b)
    else:
        for b in range(dst_blocks):
            write(out_refs[0], pl.ds(b * BLK, BLK), b)


def merge_kernel(heads, *refs):
    *part_refs, bias_ref, out_ref = refs
    width = bias_ref.shape[1]
    size = width // heads
    stats = [ref[width:].astype(f32) for ref in part_refs]
    tops = [s[:heads] + s[heads : 2 * heads] + s[2 * heads : 3 * heads] for s in stats]
    best = functools.reduce(jnp.maximum, tops)
    scales = [jnp.exp2(t - best) for t in tops]
    denom = sum(scale * s[3 * heads :] for scale, s in zip(scales, stats))
    inverse = 1.0 / jnp.maximum(denom, 1.0)
    scales = [scale * inverse for scale in scales]
    blended = []
    for h in range(heads):
        part = slice(h * size, (h + 1) * size)
        blended.append(
            sum(
                ref[part].astype(f32) * scale[h : h + 1]
                for ref, scale in zip(part_refs, scales)
            )
        )
    value = jnp.concatenate(blended, axis=0).T + bias_ref[...]
    out_ref[...] = jnp.where(value > 0, value, jnp.exp(value) - 1.0).astype(bf16)


def pairs(count, k):
    return [(i, i ^ k) for i in range(count)]


def body(
    n_row,
    n_col,
    source_features,
    target_features,
    weight,
    score_source,
    score_target,
    out_bias,
    block_list,
    block_count,
    edge_bits,
):
    heads, size = score_source.shape
    width = weight.shape[1]
    own_src = source_features.shape[1]
    own_dst = target_features.shape[0]
    src_blocks = own_src * n_row // BLK
    dst_blocks = own_dst * n_col // BLK
    split = (
        own_src % BLK == 0
        and own_dst % BLK == 0
        and n_row & (n_row - 1) == 0
        and n_col & (n_col - 1) == 0
    )
    vmem = pl.BlockSpec(memory_space=pltpu.VMEM)
    smem = pl.BlockSpec(memory_space=pltpu.SMEM)

    dst_own = pl.pallas_call(
        target_kernel,
        out_shape=jax.ShapeDtypeStruct((heads, own_dst), f32),
        in_specs=[vmem] * 3,
        out_specs=vmem,
    )(target_features, weight, score_target)

    if split:
        x = source_features
        even = [x] + [lax.ppermute(x, "row", pairs(n_row, k)) for k in range(2, n_row, 2)]
        odd = [lax.ppermute(y, "row", pairs(n_row, 1)) for y in even] if n_row > 1 else []
        xs = [y for both in zip(even, odd) for y in both] if odd else even
        ds = [dst_own] + [lax.ppermute(dst_own, "col", pairs(n_col, k)) for k in range(1, n_col)]
    else:
        xs = [lax.all_gather(source_features[0], "row", axis=0, tiled=True)]
        ds = [lax.all_gather(dst_own, "col", axis=1, tiled=True)]

    extra = 4 * heads
    if split:
        outs = [jax.ShapeDtypeStruct((width + extra, own_dst), bf16)] * n_col
    else:
        outs = [jax.ShapeDtypeStruct((width + extra, own_dst * n_col), bf16)]
    cfg = (heads, size, src_blocks, dst_blocks, len(xs), len(ds), "row", "col", split)
    chunks = pl.pallas_call(
        functools.partial(tile_kernel, cfg),
        out_shape=outs,
        in_specs=[smem, smem] + [vmem] * (3 + len(xs) + len(ds)),
        out_specs=[vmem] * len(outs),
        scratch_shapes=[
            pltpu.VMEM((src_blocks, width, BLK), bf16),
            pltpu.VMEM((src_blocks * heads, BLK, BLK), f32),
            pltpu.VMEM((dst_blocks, heads, BLK), f32),
            pltpu.VMEM((dst_blocks * heads, 8, BLK), f32),
            pltpu.VMEM((dst_blocks * heads, 8, BLK), f32),
            pltpu.VMEM((dst_blocks, width, BLK), f32),
        ],
    )(block_list, block_count, edge_bits, weight, score_source, *xs, *ds)

    if not split:
        me = lax.axis_index("col")
        chunks = [
            lax.dynamic_slice_in_dim(chunks[0], (me ^ k) * own_dst, own_dst, 1)
            for k in range(n_col)
        ]
    parts = [chunks[0]] + [
        lax.ppermute(chunks[k], "col", pairs(n_col, k)) for k in range(1, n_col)
    ]
    return pl.pallas_call(
        functools.partial(merge_kernel, heads),
        out_shape=jax.ShapeDtypeStruct((own_dst, width), bf16),
        in_specs=[vmem] * (len(parts) + 1),
        out_specs=vmem,
    )(*parts, out_bias.reshape(1, width))


def solution(mesh):
    placed = (
        P("col", "row", None),
        P(("row", "col"), None),
        P(),
        P(),
        P(),
        P(),
        P("row", "col", None),
        P("row", "col"),
        P("row", "col", None, None, None),
    )
    return jax.shard_map(
        functools.partial(body, mesh.shape["row"], mesh.shape["col"]),
        mesh=mesh,
        in_specs=placed,
        out_specs=P(("row", "col"), None),
        check_vma=False,
    )
```

time: 130 us -> 55.4 us (0.43)
  blocking collectives: 42.5 us -> 0 us
  matrix products: 20.7 us -> 0 us
  Pallas kernels: 0 us -> 16.2 us
  other arithmetic: 15.3 us -> 0 us
  starting transfers between devices: 0.04 us -> 15.2 us
  between operations: 14.3 us -> 0.74 us
  local copies, waits for them, and re-layouts: 10.9 us -> 2.04 us
  waiting for transfers between devices: 26.1 us -> 21.2 us
    psum x1 -> x0, waiting for transfers between devices: 21.7 us -> none  [body(): lax.psum(accum.astype(jnp.bfloat16), 'col').astype(jnp.float32)]
    ppermute x0 -> x13, waiting for transfers between devices: none -> 21.2 us  [the longest x3 7.79 us: body(): lax.ppermute(chunks[k], 'col', pairs(n_col, k))]
    dot_general x7 -> x0, matrix products: 20.7 us -> none  [the longest x1 9.89 us: body(): jnp.einsum('hsji,sjhk->sihk', weights, src_feats, preferred_element_type=...]
    pmax x1 -> x0, blocking collectives: 18.7 us -> none  [body(): row_max = lax.pmax(row_max, 'col')]
    pallas_call x0 -> x3, Pallas kernels: none -> 16.2 us  [the longest x1 12.1 us: body(): pl.pallas_call(functools.partial(tile_kernel, cfg), out_shape=outs, in_sp...]
    ppermute x0 -> x13, starting transfers between devices: none -> 15.2 us  [the longest x3 6.31 us: body(): lax.ppermute(dst_own, 'col', pairs(n_col, k))]
    all_gather x1 -> x0, blocking collectives: 14.9 us -> none  [body(): dst_logits = lax.all_gather(dst_local, 'col', axis=1, tiled=True)]
    psum x1 -> x0, blocking collectives: 8.82 us -> none  [body(): lax.psum(denoms.astype(jnp.bfloat16), 'col').astype(jnp.float32)]
  transfers between devices with their start and end apart: 2 -> 13, of which waited for: 2 -> 8; matrix products, arithmetic and copies ran while one was open for 9% -> 0% of each run, Pallas kernels for 0% -> 4%
where the time goes in v1:
time: 55.4 us; the launch traced here: 55.3 us
  waiting for transfers between devices  21.2 us (38%)
  Pallas kernels  16.2 us (29%)
  starting transfers between devices  15.2 us (27%)
  local copies, waits for them, and re-layouts  2.04 us (4%)
  between operations  0.74 us (1%)
    pallas_call x1, Pallas kernels, body(): pl.pallas_call(functools.partial(tile_kernel, cfg), out_shape=outs, in_sp...  12.1 us
    ppermute x3, waiting for transfers between devices, body(): lax.ppermute(chunks[k], 'col', pairs(n_col, k))  7.79 us
    ppermute x3, waiting for transfers between devices, body(): lax.ppermute(dst_own, 'col', pairs(n_col, k))  7.2 us
    ppermute x3, starting transfers between devices, body(): lax.ppermute(dst_own, 'col', pairs(n_col, k))  6.31 us
    ppermute x3, waiting for transfers between devices, body(): lax.ppermute(x, 'row', pairs(n_row, k))  6.19 us
    ppermute x3, starting transfers between devices, body(): lax.ppermute(x, 'row', pairs(n_row, k))  4.49 us
    ppermute x3, starting transfers between devices, body(): lax.ppermute(chunks[k], 'col', pairs(n_col, k))  4.38 us
    pallas_call x1, Pallas kernels, body(): pl.pallas_call(target_kernel, out_shape=jax.ShapeDtypeStruct((heads, own_...  2.08 us
  transfers between devices with their start and end apart: 13, of which 8 were waited for; matrix products, arithmetic and copies ran while one was open for 0% of the time, Pallas kernels for 4%

profile of v1, /device:TPU:0, one launch (start us, length us, event | category | flops | bytes accessed | tf_op | source)
XLA Modules:
  0.0 55.3 jit_solution(6399087150654993505)
XLA Ops:
  0.0 3.0 %collective-permute-start.3 = (bf16[1,256,256]{2,1,0:T(8,128)(2,1)}, bf16[1,256,256]{2,1,0:T(8,128)(2,1)S(1)}, u32[]{:S(2)}, u32[]{:S(2)}) collective-permute-start(bf16[1,256,256]{2,1,0:T(8,128)(2,1)} %refs_5_.1), channel_id=1, source_target_pairs={{0,16},{4,20},{8,24},{12,28},{16,0},{20,4},{24,8},{28,12},{1,17},{... | collective-permute-start | bytes 393224 | tf_op jit(solution)/shard_map/ppermute | solution.py:237
  3.0 1.5 %collective-permute-start.1 = (bf16[1,256,256]{2,1,0:T(8,128)(2,1)}, bf16[1,256,256]{2,1,0:T(8,128)(2,1)S(1)}, u32[]{:S(2)}, u32[]{:S(2)}) collective-permute-start(bf16[1,256,256]{2,1,0:T(8,128)(2,1)} %refs_5_.1), channel_id=1, source_target_pairs={{0,8},{4,12},{8,0},{12,4},{16,24},{20,28},{24,16},{28,20},{1,9},{5... | collective-permute-start | bytes 393224 | tf_op jit(solution)/shard_map/ppermute | solution.py:237
  4.5 0.0 collective-permute-start.5
  4.5 0.0 collective-permute-start
  4.5 2.2 %collective-permute-done.3.refs_9_ = bf16[1,256,256]{2,1,0:T(8,128)(2,1)S(1)} collective-permute-done((bf16[1,256,256]{2,1,0:T(8,128)(2,1)}, bf16[1,256,256]{2,1,0:T(8,128)(2,1)S(1)}, u32[]{:S(2)}, u32[]{:S(2)}) %collective-permute-start.3) | collective-permute-done | bytes 131104 | tf_op jit(solution)/shard_map/ppermute | solution.py:237
  6.7 0.0 copy-start.3
  6.7 0.0 collective-permute-start.4
  6.7 2.9 %collective-permute-done.1.refs_7_ = bf16[1,256,256]{2,1,0:T(8,128)(2,1)S(1)} collective-permute-done((bf16[1,256,256]{2,1,0:T(8,128)(2,1)}, bf16[1,256,256]{2,1,0:T(8,128)(2,1)S(1)}, u32[]{:S(2)}, u32[]{:S(2)}) %collective-permute-start.1) | collective-permute-done | bytes 131104 | tf_op jit(solution)/shard_map/ppermute | solution.py:237
  9.6 0.0 copy-start.4
  9.6 0.0 collective-permute-start.2
  9.6 1.1 %collective-permute-done.5.refs_11_ = bf16[1,256,256]{2,1,0:T(8,128)(2,1)S(1)} collective-permute-done((bf16[1,256,256]{2,1,0:T(8,128)(2,1)}, bf16[1,256,256]{2,1,0:T(8,128)(2,1)S(1)}, u32[]{:S(2)}, u32[]{:S(2)}) %collective-permute-start.5) | collective-permute-done | bytes 131104 | tf_op jit(solution)/shard_map/ppermute | solution.py:237
  10.7 0.0 copy-start.5
  10.7 0.0 collective-permute-start.6
  10.7 2.1 %shard_map.91.refs_13_ = f32[4,256]{1,0:T(4,128)} custom-call(bf16[256,256]{1,0:T(8,128)(2,1)} %x_ref.1, bf16[256,256]{1,0:T(8,128)(2,1)} %refs_3_.1, f32[4,64]{1,0:T(4,128)} %score_ref.1), custom_call_target="tpu_custom_call" | custom-call | tf_op jit(solution)/shard_map/pallas_call | solution.py:228
  12.8 0.0 copy-done.3
  12.8 0.0 copy-done.4
  12.8 3.8 %collective-permute-start.9 = (f32[4,256]{1,0:T(4,128)}, f32[4,256]{1,0:T(4,128)S(1)}, u32[]{:S(2)}, u32[]{:S(2)}) collective-permute-start(f32[4,256]{1,0:T(4,128)} %shard_map.91.refs_13_), channel_id=1, source_target_pairs={{0,3},{1,2},{2,1},{3,0},{4,7},{5,6},{6,5},{7,4},{8,11},{9,10},{10,... | collective-permute-start | bytes 12296 | tf_op jit(solution)/shard_map/ppermute | solution.py:240
  16.6 1.8 %collective-permute-done.9.refs_16_ = f32[4,256]{1,0:T(4,128)S(1)} collective-permute-done((f32[4,256]{1,0:T(4,128)}, f32[4,256]{1,0:T(4,128)S(1)}, u32[]{:S(2)}, u32[]{:S(2)}) %collective-permute-start.9) | collective-permute-done | bytes 4128 | tf_op jit(solution)/shard_map/ppermute | solution.py:240
  18.4 0.0 copy-start.10
  18.4 1.0 %collective-permute-start.8 = (f32[4,256]{1,0:T(4,128)}, f32[4,256]{1,0:T(4,128)S(1)}, u32[]{:S(2)}, u32[]{:S(2)}) collective-permute-start(f32[4,256]{1,0:T(4,128)} %shard_map.91.refs_13_), channel_id=1, source_target_pairs={{0,2},{1,3},{2,0},{3,1},{4,6},{5,7},{6,4},{7,5},{8,10},{9,11},{10,... | collective-permute-start | bytes 12296 | tf_op jit(solution)/shard_map/ppermute | solution.py:240
  19.4 3.7 %collective-permute-done.8.refs_15_ = f32[4,256]{1,0:T(4,128)S(1)} collective-permute-done((f32[4,256]{1,0:T(4,128)}, f32[4,256]{1,0:T(4,128)S(1)}, u32[]{:S(2)}, u32[]{:S(2)}) %collective-permute-start.8) | collective-permute-done | bytes 4128 | tf_op jit(solution)/shard_map/ppermute | solution.py:240
  23.1 0.0 copy-start.11
  23.1 1.5 %collective-permute-start.7 = (f32[4,256]{1,0:T(4,128)}, f32[4,256]{1,0:T(4,128)S(1)}, u32[]{:S(2)}, u32[]{:S(2)}) collective-permute-start(f32[4,256]{1,0:T(4,128)} %shard_map.91.refs_13_), channel_id=1, source_target_pairs={{0,1},{1,0},{2,3},{3,2},{4,5},{5,4},{6,7},{7,6},{8,9},{9,8},{10,11... | collective-permute-start | bytes 12296 | tf_op jit(solution)/shard_map/ppermute | solution.py:240
  25.3 1.7 %collective-permute-done.7.refs_14_ = f32[4,256]{1,0:T(4,128)S(1)} collective-permute-done((f32[4,256]{1,0:T(4,128)}, f32[4,256]{1,0:T(4,128)S(1)}, u32[]{:S(2)}, u32[]{:S(2)}) %collective-permute-start.7) | collective-permute-done | bytes 4128 | tf_op jit(solution)/shard_map/ppermute | solution.py:240
  27.0 0.0 copy-start.12
  27.0 0.0 collective-permute-done.refs_6_
  27.0 0.0 copy-start.6
  27.0 0.0 collective-permute-done.4.refs_10_
  27.0 0.0 copy-start.7
  27.0 0.0 collective-permute-done.2.refs_8_
  27.0 0.0 copy-start.8
  27.0 0.0 collective-permute-done.6.refs_12_
  27.0 0.0 copy-done.5
  27.0 0.0 copy-done.10
  27.0 0.0 copy-done.11
  27.0 0.5 copy-done.12
  27.6 0.1 copy-done.6
  27.6 0.0 copy-done.7
  27.7 0.0 copy-done.8
  27.7 0.0 copy-start.9
  27.7 0.7 %copy-done.9 = bf16[1,256,256]{2,1,0:T(8,128)(2,1)} copy-done((bf16[1,256,256]{2,1,0:T(8,128)(2,1)}, bf16[1,256,256]{2,1,0:T(8,128)(2,1)S(1)}, u32[]{:S(2)}) %copy-start.9) | copy-done | bytes 131096
  28.4 12.1 %shard_map.92 = (bf16[272,256]{1,0:T(8,128)(2,1)}, bf16[272,256]{1,0:T(8,128)(2,1)}, bf16[272,256]{1,0:T(8,128)(2,1)}, bf16[272,256]{1,0:T(8,128)(2,1)}) custom-call(s32[1,1,48]{2,1,0:T(1,128)} %refs_0_.1, s32[1,1]{1,0:T(1,128)S(6)} %copy.10.refs_1_, s32[1,1,48,16,128]{4,3,2,1,0:T(8,128)} %refs_2_.1, bf16[256,256]{1,0:T(8,128)(2,1)} %refs_3_.1, ...), custom_call_target="tpu_custom_call" | custom-call | tf_op jit(solution)/shard_map/pallas_call | solution.py:251
  40.5 0.0 collective-permute-start.10
  40.5 0.6 %collective-permute-start.11 = (bf16[272,256]{1,0:T(8,128)(2,1)}, bf16[272,256]{1,0:T(8,128)(2,1)S(1)}, u32[]{:S(2)}, u32[]{:S(2)}) collective-permute-start(bf16[272,256]{1,0:T(8,128)(2,1)} %get-tuple-element.11), channel_id=1, source_target_pairs={{0,2},{1,3},{2,0},{3,1},{4,6},{5,7},{6,4},{7,5},{8,10},{9,11},{10,... | collective-permute-start | bytes 417800 | tf_op jit(solution)/shard_map/ppermute | solution.py:273
  41.1 3.8 %collective-permute-start.12 = (bf16[272,256]{1,0:T(8,128)(2,1)}, bf16[272,256]{1,0:T(8,128)(2,1)S(1)}, u32[]{:S(2)}, u32[]{:S(2)}) collective-permute-start(bf16[272,256]{1,0:T(8,128)(2,1)} %get-tuple-element.12), channel_id=1, source_target_pairs={{0,3},{1,2},{2,1},{3,0},{4,7},{5,6},{6,5},{7,4},{8,11},{9,10},{10,... | collective-permute-start | bytes 417800 | tf_op jit(solution)/shard_map/ppermute | solution.py:273
  44.9 0.9 %collective-permute-done.10.refs_1_ = bf16[272,256]{1,0:T(8,128)(2,1)S(1)} collective-permute-done((bf16[272,256]{1,0:T(8,128)(2,1)}, bf16[272,256]{1,0:T(8,128)(2,1)S(1)}, u32[]{:S(2)}, u32[]{:S(2)}) %collective-permute-start.10) | collective-permute-done | bytes 139296 | tf_op jit(solution)/shard_map/ppermute | solution.py:273
  45.8 0.0 copy-start
  45.8 6.8 %collective-permute-done.11.refs_2_ = bf16[272,256]{1,0:T(8,128)(2,1)S(1)} collective-permute-done((bf16[272,256]{1,0:T(8,128)(2,1)}, bf16[272,256]{1,0:T(8,128)(2,1)S(1)}, u32[]{:S(2)}, u32[]{:S(2)}) %collective-permute-start.11) | collective-permute-done | bytes 139296 | tf_op jit(solution)/shard_map/ppermute | solution.py:273
  52.6 0.0 copy-start.1
  52.6 0.0 collective-permute-done.12.refs_3_
  52.7 0.0 copy-start.2
  52.7 0.0 copy-done
  52.7 0.6 %copy-done.1 = bf16[272,256]{1,0:T(8,128)(2,1)} copy-done((bf16[272,256]{1,0:T(8,128)(2,1)}, bf16[272,256]{1,0:T(8,128)(2,1)S(1)}, u32[]{:S(2)}) %copy-start.1) | copy-done | bytes 139288
  53.3 0.1 copy-done.2
  53.4 2.0 %shard_map.93 = bf16[256,256]{1,0:T(8,128)(2,1)} custom-call(bf16[272,256]{1,0:T(8,128)(2,1)} %get-tuple-element.9.refs_0_, bf16[272,256]{1,0:T(8,128)(2,1)} %copy-done, bf16[272,256]{1,0:T(8,128)(2,1)} %copy-done.1, bf16[272,256]{1,0:T(8,128)(2,1)} %copy-done.2, f32[1,256]{1,0:T(1,128)} %bitcast.1), custom_call_target="tpu_custom_call" | custom-call | tf_op jit(solution)/shard_map/pallas_call | solution.py:275
Async XLA Ops:
  0.0 6.7 %collective-permute-start.3 = (bf16[1,256,256]{2,1,0:T(8,128)(2,1)}, bf16[1,256,256]{2,1,0:T(8,128)(2,1)S(1)}, u32[]{:S(2)}, u32[]{:S(2)}) collective-permute-start(bf16[1,256,256]{2,1,0:T(8,128)(2,1)} %refs_5_.1), channel_id=1, source_target_pairs={{0,16},{4,20},{8,24},{12,28},{16,0},{20,4},{24,8},{28,12},{1,17},{... | collective-permute-start | bytes 393224 | tf_op jit(solution)/shard_map/ppermute | solution.py:237
  3.0 6.6 %collective-permute-start.1 = (bf16[1,256,256]{2,1,0:T(8,128)(2,1)}, bf16[1,256,256]{2,1,0:T(8,128)(2,1)S(1)}, u32[]{:S(2)}, u32[]{:S(2)}) collective-permute-start(bf16[1,256,256]{2,1,0:T(8,128)(2,1)} %refs_5_.1), channel_id=1, source_target_pairs={{0,8},{4,12},{8,0},{12,4},{16,24},{20,28},{24,16},{28,20},{1,9},{5... | collective-permute-start | bytes 393224 | tf_op jit(solution)/shard_map/ppermute | solution.py:237
  4.5 6.2 %collective-permute-start.5 = (bf16[1,256,256]{2,1,0:T(8,128)(2,1)}, bf16[1,256,256]{2,1,0:T(8,128)(2,1)S(1)}, u32[]{:S(2)}, u32[]{:S(2)}) collective-permute-start(bf16[1,256,256]{2,1,0:T(8,128)(2,1)} %refs_5_.1), channel_id=1, source_target_pairs={{0,24},{4,28},{8,16},{12,20},{16,8},{20,12},{24,0},{28,4},{1,25},{... | collective-permute-start | bytes 393224 | tf_op jit(solution)/shard_map/ppermute | solution.py:237
  4.5 22.5 %collective-permute-start = (bf16[1,256,256]{2,1,0:T(8,128)(2,1)}, bf16[1,256,256]{2,1,0:T(8,128)(2,1)S(1)}, u32[]{:S(2)}, u32[]{:S(2)}) collective-permute-start(bf16[1,256,256]{2,1,0:T(8,128)(2,1)} %refs_5_.1), channel_id=1, source_target_pairs={{0,4},{4,0},{8,12},{12,8},{16,20},{20,16},{24,28},{28,24},{1,5},{5... | collective-permute-start | bytes 393224 | tf_op jit(solution)/shard_map/ppermute | solution.py:238
  6.7 6.1 %copy-start.3 = (bf16[1,256,256]{2,1,0:T(8,128)(2,1)}, bf16[1,256,256]{2,1,0:T(8,128)(2,1)S(1)}, u32[]{:S(2)}) copy-start(bf16[1,256,256]{2,1,0:T(8,128)(2,1)S(1)} %collective-permute-done.3.refs_9_) | copy-start | bytes 393220
  6.7 20.3 %collective-permute-start.4 = (bf16[1,256,256]{2,1,0:T(8,128)(2,1)S(1)}, bf16[1,256,256]{2,1,0:T(8,128)(2,1)S(1)}, u32[]{:S(2)}, u32[]{:S(2)}) collective-permute-start(bf16[1,256,256]{2,1,0:T(8,128)(2,1)S(1)} %collective-permute-done.3.refs_9_), channel_id=1, source_target_pairs={{0,4},{4,0},{8,12},{12,8},{16,20},{20,16},{24,28},{28,24},{1,5},{5... | collective-permute-start | bytes 393224 | tf_op jit(solution)/shard_map/ppermute | solution.py:238
  9.6 3.2 %copy-start.4 = (bf16[1,256,256]{2,1,0:T(8,128)(2,1)}, bf16[1,256,256]{2,1,0:T(8,128)(2,1)S(1)}, u32[]{:S(2)}) copy-start(bf16[1,256,256]{2,1,0:T(8,128)(2,1)S(1)} %collective-permute-done.1.refs_7_) | copy-start | bytes 393220
  9.6 17.4 %collective-permute-start.2 = (bf16[1,256,256]{2,1,0:T(8,128)(2,1)S(1)}, bf16[1,256,256]{2,1,0:T(8,128)(2,1)S(1)}, u32[]{:S(2)}, u32[]{:S(2)}) collective-permute-start(bf16[1,256,256]{2,1,0:T(8,128)(2,1)S(1)} %collective-permute-done.1.refs_7_), channel_id=1, source_target_pairs={{0,4},{4,0},{8,12},{12,8},{16,20},{20,16},{24,28},{28,24},{1,5},{5... | collective-permute-start | bytes 393224 | tf_op jit(solution)/shard_map/ppermute | solution.py:238
  10.7 16.3 %copy-start.5 = (bf16[1,256,256]{2,1,0:T(8,128)(2,1)}, bf16[1,256,256]{2,1,0:T(8,128)(2,1)S(1)}, u32[]{:S(2)}) copy-start(bf16[1,256,256]{2,1,0:T(8,128)(2,1)S(1)} %collective-permute-done.5.refs_11_) | copy-start | bytes 393220
  10.7 16.3 %collective-permute-start.6 = (bf16[1,256,256]{2,1,0:T(8,128)(2,1)S(1)}, bf16[1,256,256]{2,1,0:T(8,128)(2,1)S(1)}, u32[]{:S(2)}, u32[]{:S(2)}) collective-permute-start(bf16[1,256,256]{2,1,0:T(8,128)(2,1)S(1)} %collective-permute-done.5.refs_11_), channel_id=1, source_target_pairs={{0,4},{4,0},{8,12},{12,8},{16,20},{20,16},{24,28},{28,24},{1,5},{5... | collective-permute-start | bytes 393224 | tf_op jit(solution)/shard_map/ppermute | solution.py:238
  12.8 5.6 %collective-permute-start.9 = (f32[4,256]{1,0:T(4,128)}, f32[4,256]{1,0:T(4,128)S(1)}, u32[]{:S(2)}, u32[]{:S(2)}) collective-permute-start(f32[4,256]{1,0:T(4,128)} %shard_map.91.refs_13_), channel_id=1, source_target_pairs={{0,3},{1,2},{2,1},{3,0},{4,7},{5,6},{6,5},{7,4},{8,11},{9,10},{10,... | collective-permute-start | bytes 12296 | tf_op jit(solution)/shard_map/ppermute | solution.py:240
  18.4 8.6 %copy-start.10 = (f32[4,256]{1,0:T(4,128)}, f32[4,256]{1,0:T(4,128)S(1)}, u32[]{:S(2)}) copy-start(f32[4,256]{1,0:T(4,128)S(1)} %collective-permute-done.9.refs_16_) | copy-start | bytes 12292
  18.4 4.7 %collective-permute-start.8 = (f32[4,256]{1,0:T(4,128)}, f32[4,256]{1,0:T(4,128)S(1)}, u32[]{:S(2)}, u32[]{:S(2)}) collective-permute-start(f32[4,256]{1,0:T(4,128)} %shard_map.91.refs_13_), channel_id=1, source_target_pairs={{0,2},{1,3},{2,0},{3,1},{4,6},{5,7},{6,4},{7,5},{8,10},{9,11},{10,... | collective-permute-start | bytes 12296 | tf_op jit(solution)/shard_map/ppermute | solution.py:240
  23.1 3.9 %copy-start.11 = (f32[4,256]{1,0:T(4,128)}, f32[4,256]{1,0:T(4,128)S(1)}, u32[]{:S(2)}) copy-start(f32[4,256]{1,0:T(4,128)S(1)} %collective-permute-done.8.refs_15_) | copy-start | bytes 12292
  23.1 3.8 %collective-permute-start.7 = (f32[4,256]{1,0:T(4,128)}, f32[4,256]{1,0:T(4,128)S(1)}, u32[]{:S(2)}, u32[]{:S(2)}) collective-permute-start(f32[4,256]{1,0:T(4,128)} %shard_map.91.refs_13_), channel_id=1, source_target_pairs={{0,1},{1,0},{2,3},{3,2},{4,5},{5,4},{6,7},{7,6},{8,9},{9,8},{10,11... | collective-permute-start | bytes 12296 | tf_op jit(solution)/shard_map/ppermute | solution.py:240
  27.0 0.6 %copy-start.12 = (f32[4,256]{1,0:T(4,128)}, f32[4,256]{1,0:T(4,128)S(1)}, u32[]{:S(2)}) copy-start(f32[4,256]{1,0:T(4,128)S(1)} %collective-permute-done.7.refs_14_) | copy-start | bytes 12292
  27.0 0.7 %copy-start.6 = (bf16[1,256,256]{2,1,0:T(8,128)(2,1)}, bf16[1,256,256]{2,1,0:T(8,128)(2,1)S(1)}, u32[]{:S(2)}) copy-start(bf16[1,256,256]{2,1,0:T(8,128)(2,1)S(1)} %collective-permute-done.refs_6_) | copy-start | bytes 393220
  27.0 0.7 %copy-start.7 = (bf16[1,256,256]{2,1,0:T(8,128)(2,1)}, bf16[1,256,256]{2,1,0:T(8,128)(2,1)S(1)}, u32[]{:S(2)}) copy-start(bf16[1,256,256]{2,1,0:T(8,128)(2,1)S(1)} %collective-permute-done.4.refs_10_) | copy-start | bytes 393220
  27.0 0.7 %copy-start.8 = (bf16[1,256,256]{2,1,0:T(8,128)(2,1)}, bf16[1,256,256]{2,1,0:T(8,128)(2,1)S(1)}, u32[]{:S(2)}) copy-start(bf16[1,256,256]{2,1,0:T(8,128)(2,1)S(1)} %collective-permute-done.2.refs_8_) | copy-start | bytes 393220
  27.7 0.7 %copy-start.9 = (bf16[1,256,256]{2,1,0:T(8,128)(2,1)}, bf16[1,256,256]{2,1,0:T(8,128)(2,1)S(1)}, u32[]{:S(2)}) copy-start(bf16[1,256,256]{2,1,0:T(8,128)(2,1)S(1)} %collective-permute-done.6.refs_12_) | copy-start | bytes 393220
  40.5 5.3 %collective-permute-start.10 = (bf16[272,256]{1,0:T(8,128)(2,1)}, bf16[272,256]{1,0:T(8,128)(2,1)S(1)}, u32[]{:S(2)}, u32[]{:S(2)}) collective-permute-start(bf16[272,256]{1,0:T(8,128)(2,1)} %get-tuple-element.10), channel_id=1, source_target_pairs={{0,1},{1,0},{2,3},{3,2},{4,5},{5,4},{6,7},{7,6},{8,9},{9,8},{10,11... | collective-permute-start | bytes 417800 | tf_op jit(solution)/shard_map/ppermute | solution.py:273
  40.5 12.2 %collective-permute-start.11 = (bf16[272,256]{1,0:T(8,128)(2,1)}, bf16[272,256]{1,0:T(8,128)(2,1)S(1)}, u32[]{:S(2)}, u32[]{:S(2)}) collective-permute-start(bf16[272,256]{1,0:T(8,128)(2,1)} %get-tuple-element.11), channel_id=1, source_target_pairs={{0,2},{1,3},{2,0},{3,1},{4,6},{5,7},{6,4},{7,5},{8,10},{9,11},{10,... | collective-permute-start | bytes 417800 | tf_op jit(solution)/shard_map/ppermute | solution.py:273
  41.1 11.6 %collective-permute-start.12 = (bf16[272,256]{1,0:T(8,128)(2,1)}, bf16[272,256]{1,0:T(8,128)(2,1)S(1)}, u32[]{:S(2)}, u32[]{:S(2)}) collective-permute-start(bf16[272,256]{1,0:T(8,128)(2,1)} %get-tuple-element.12), channel_id=1, source_target_pairs={{0,3},{1,2},{2,1},{3,0},{4,7},{5,6},{6,5},{7,4},{8,11},{9,10},{10,... | collective-permute-start | bytes 417800 | tf_op jit(solution)/shard_map/ppermute | solution.py:273
  45.8 6.9 %copy-start = (bf16[272,256]{1,0:T(8,128)(2,1)}, bf16[272,256]{1,0:T(8,128)(2,1)S(1)}, u32[]{:S(2)}) copy-start(bf16[272,256]{1,0:T(8,128)(2,1)S(1)} %collective-permute-done.10.refs_1_) | copy-start | bytes 417796
  52.6 0.7 %copy-start.1 = (bf16[272,256]{1,0:T(8,128)(2,1)}, bf16[272,256]{1,0:T(8,128)(2,1)S(1)}, u32[]{:S(2)}) copy-start(bf16[272,256]{1,0:T(8,128)(2,1)S(1)} %collective-permute-done.11.refs_2_) | copy-start | bytes 417796
  52.7 0.7 %copy-start.2 = (bf16[272,256]{1,0:T(8,128)(2,1)}, bf16[272,256]{1,0:T(8,128)(2,1)S(1)}, u32[]{:S(2)}) copy-start(bf16[272,256]{1,0:T(8,128)(2,1)S(1)} %collective-permute-done.12.refs_3_) | copy-start | bytes 417796
